TPU v7x, 32 devices: a whole 2x2x4 slice. The times are simulated.
32 devices in a mesh: group: 2 (over y), seq: 4 (over z), req: 2 (over x), sub: 2 (over core).
Axes of the slice: x: 2, y: 2, z: 4, core: 2. Of those that a mesh axis runs over, the one named last changes fastest.
Arguments:
- latent_codes: bfloat16 [2, 16, 2048, 512], P(None, ('group', 'req', 'sub'), 'seq'), parts along dimension 1, may hold values from -6 to 6
- latent_scales: bfloat16 [2, 16, 2048, 4], P(None, ('group', 'req', 'sub'), 'seq'), parts along dimension 1, may hold values from 0.34 to 3.5
- rope_keys: bfloat16 [2, 16, 2048, 64], P(None, ('group', 'req', 'sub'), 'seq'), parts along dimension 1, may hold values from -6 to 6
- lengths: int32 [16], P(('group', 'req', 'sub')), parts along dimension 0, may hold values from 256 to 2048, as said below
- query_latent: bfloat16 [2, 16, 4, 128, 512], P(None, ('group', 'req', 'sub'), None, 'seq'), parts along dimension 1, may hold values from -64 to 64
- query_rope: bfloat16 [2, 16, 4, 128, 64], P(None, ('group', 'req', 'sub'), None, 'seq'), parts along dimension 1, may hold values from -8 to 8
- new_latent: bfloat16 [2, 16, 4, 512], P(None, ('group', 'req', 'sub')), parts along dimension 1, may hold values from -9 to 9
- new_rope: bfloat16 [2, 16, 4, 64], P(None, ('group', 'req', 'sub')), parts along dimension 1, may hold values from -6 to 6
Outputs:
- attended: bfloat16 [2, 16, 4, 128, 512], P(None, ('group', 'req', 'sub'), None, 'seq'), parts along dimension 1
- cache_codes: bfloat16 [2, 16, 512, 4, 512], P(None, ('group', 'req', 'sub'), None, 'seq'), parts along dimension 1
- cache_scales: bfloat16 [2, 16, 512, 4, 4], P(None, ('group', 'req', 'sub'), None, 'seq'), parts along dimension 1
- cache_rope: bfloat16 [2, 16, 512, 4, 64], P(None, ('group', 'req', 'sub'), None, 'seq'), parts along dimension 1
There are 2 independent parts, one for each index of `group`. A program takes and returns all parts, laid end to end along the dimension named above; each array names one. Nothing has to cross between parts.
Inputs may be any that keep to these rules, and one draw needn't show every extreme that they name: `lengths`: one request is exactly 2048 long.
All inputs are finite; a program needn't handle non-finite values.
Results may differ from a plain program's by a relative error of at most 0.013.
Values may be sent and summed in bfloat16 or wider, within the bound.
A program may use at most 64 MiB of HBM per device.

v0:
```python
import jax
import jax.numpy as jnp
from jax import lax
from jax.sharding import PartitionSpec as P

softmax_gain = 192.0 ** (-0.5)
masked_score = -1e30


def dequantize(code_values, scale_values):
    blocks = scale_values.shape[-1]
    latent_width = code_values.shape[-1]
    shaped = code_values.astype(jnp.float32).reshape(
        code_values.shape[:-1] + (blocks, latent_width // blocks)
    )
    scaled = shaped * scale_values.astype(jnp.float32)[..., None]
    return scaled.reshape(code_values.shape).astype(jnp.bfloat16)


def shard_partial(
    lat_query, rope_query, key_rows, rope_rows, usable, new_keys, new_rope_rows, holds_new
):
    tokens_new, head_count, latent_width = lat_query.shape
    query_rows = lat_query.reshape(tokens_new * head_count, latent_width)
    query_pos = rope_query.reshape(tokens_new * head_count, rope_query.shape[-1])
    scores = jnp.dot(query_rows, key_rows.T, preferred_element_type=jnp.float32)
    scores = (
        scores + jnp.dot(query_pos, rope_rows.T, preferred_element_type=jnp.float32)
    ) * softmax_gain
    fresh_scores = jnp.dot(query_rows, new_keys.T, preferred_element_type=jnp.float32)
    fresh_scores = (
        fresh_scores + jnp.dot(query_pos, new_rope_rows.T, preferred_element_type=jnp.float32)
    ) * softmax_gain
    token_of_row = jnp.arange(tokens_new * head_count, dtype=jnp.int32) // head_count
    causal = (jnp.arange(tokens_new, dtype=jnp.int32)[None, :] <= token_of_row[:, None]) & holds_new
    scores = jnp.where(usable[None, :], scores, masked_score)
    fresh_scores = jnp.where(causal, fresh_scores, masked_score)
    group_peak = jnp.maximum(jnp.max(scores, 1), jnp.max(fresh_scores, 1)).astype(jnp.bfloat16)
    peak_float = group_peak.astype(jnp.float32)[:, None]
    weights = jnp.where(usable[None, :], jnp.exp(scores - peak_float), 0.0).astype(jnp.bfloat16)
    fresh_weights = jnp.where(causal, jnp.exp(fresh_scores - peak_float), 0.0).astype(jnp.bfloat16)
    group_total = jnp.sum(weights.astype(jnp.float32), 1) + jnp.sum(
        fresh_weights.astype(jnp.float32), 1
    )
    group_sum = jnp.dot(weights, key_rows, preferred_element_type=jnp.float32)
    group_sum = group_sum + jnp.dot(fresh_weights, new_keys, preferred_element_type=jnp.float32)
    return (
        group_sum.astype(jnp.bfloat16).reshape(tokens_new, head_count, latent_width),
        group_peak.reshape(tokens_new, head_count),
        group_total.astype(jnp.bfloat16).reshape(tokens_new, head_count),
    )


def merge_groups(pieces):
    group_sum, group_peak, group_total = pieces
    peak_float = group_peak.astype(jnp.float32)
    overall = jnp.max(peak_float, 0)
    factor = jnp.exp(peak_float - overall)
    numerator = jnp.sum(factor[..., None] * group_sum.astype(jnp.float32), 0)
    denominator = jnp.sum(factor * group_total.astype(jnp.float32), 0)
    return (numerator / denominator[..., None]).astype(jnp.bfloat16)


def per_device(
    latent_codes, latent_scales, rope_keys, lengths, query_latent, query_rope, new_latent, new_rope
):
    shard_count = lax.axis_size("seq")
    seq_index = lax.axis_index("seq")
    layer_count, request_count, span, latent_width = latent_codes.shape
    lat_query, rope_query = (
        lax.all_gather(query_latent, "seq", axis=3, tiled=True),
        lax.all_gather(query_rope, "seq", axis=3, tiled=True),
    )

    def regroup_rows(values):
        return values.reshape(
            values.shape[0], values.shape[1], span // shard_count, shard_count, values.shape[-1]
        )

    codes_moved, scales_moved, rope_moved = (
        lax.all_to_all(regroup_rows(latent_codes), "seq", split_axis=3, concat_axis=2, tiled=True),
        lax.all_to_all(regroup_rows(latent_scales), "seq", split_axis=3, concat_axis=2, tiled=True),
        lax.all_to_all(regroup_rows(rope_keys), "seq", split_axis=3, concat_axis=2, tiled=True),
    )
    offsets = jnp.arange(span, dtype=jnp.int32)
    key_rows = dequantize(latent_codes, latent_scales)
    positions = seq_index * span + offsets
    usable = positions[None, :] < lengths[:, None]
    holds_new = seq_index == 0
    per_request = jax.vmap(shard_partial, in_axes=(0, 0, 0, 0, 0, 0, 0, None))
    per_layer = jax.vmap(per_request, in_axes=(0, 0, 0, 0, None, 0, 0, None))
    group_sum, group_peak, group_total = per_layer(
        lat_query, rope_query, key_rows, rope_keys, usable, new_latent, new_rope, holds_new
    )
    attended = merge_groups(
        (
            lax.all_to_all(group_sum[None], "seq", split_axis=4, concat_axis=0, tiled=True),
            lax.all_to_all(group_peak[None], "seq", split_axis=4, concat_axis=0, tiled=True),
            lax.all_to_all(group_total[None], "seq", split_axis=4, concat_axis=0, tiled=True),
        )
    )
    return (attended, codes_moved, scales_moved, rope_moved)


def solution(mesh):
    placed = (
        P(None, ("group", "req", "sub"), "seq", None),
        P(None, ("group", "req", "sub"), "seq", None),
        P(None, ("group", "req", "sub"), "seq", None),
        P(("group", "req", "sub")),
        P(None, ("group", "req", "sub"), None, "seq", None),
        P(None, ("group", "req", "sub"), None, "seq", None),
        P(None, ("group", "req", "sub"), None, None),
        P(None, ("group", "req", "sub"), None, None),
    )
    return jax.shard_map(
        per_device,
        mesh=mesh,
        in_specs=placed,
        out_specs=(
            P(None, ("group", "req", "sub"), None, "seq", None),
            P(None, ("group", "req", "sub"), None, "seq", None),
            P(None, ("group", "req", "sub"), None, "seq", None),
            P(None, ("group", "req", "sub"), None, "seq", None),
        ),
        check_vma=False,
    )
```

profile of v0, /device:TPU:0, one launch (start us, length us, event | category | flops | bytes accessed | tf_op | source)
XLA Modules:
  0.0 215.6 jit_solution(11127280630018597931)
XLA Ops:
  7.2 0.0 copy-start
  7.2 0.0 all-gather.2.cloned.1.call-start
  7.2 0.7 all-gather.2.cloned.1.call-update
  7.9 1.8 reshape.126
  9.8 0.8 copy.66
  10.6 6.3 %all-to-all-start.4 = ((bf16[2,2,128,4,4]{2,4,1,0,3:T(4,128)(2,1)}), bf16[2,2,128,4,4]{2,4,1,0,3:T(4,128)(2,1)S(1)}, u32[]{:S(2)}, u32[]{:S(2)}) async-start(bf16[2,2,128,4,4]{2,4,1,0,3:T(4,128)(2,1)} %copy.66), calls=%async_computation.4 | async-start | bytes 32768 | tf_op jit(solution)/shard_map/all_to_all | solution.py:82
  16.9 1.2 copy.68
  18.1 1.0 copy.69
  19.2 3.4 %all-to-all-done.4 = bf16[2,2,128,4,4]{2,4,1,0,3:T(4,128)(2,1)S(1)} async-done(((bf16[2,2,128,4,4]{2,4,1,0,3:T(4,128)(2,1)}), bf16[2,2,128,4,4]{2,4,1,0,3:T(4,128)(2,1)S(1)}, u32[]{:S(2)}, u32[]{:S(2)}) %all-to-all-start.4) | async-done | bytes 16416 | tf_op jit(solution)/shard_map/all_to_all | solution.py:82
  22.5 3.4 %all-to-all-start.5 = ((bf16[2,2,128,4,64]{2,4,1,0,3:T(8,128)(2,1)}), bf16[2,2,128,4,64]{2,4,1,0,3:T(8,128)(2,1)S(1)}, u32[]{:S(2)}, u32[]{:S(2)}) async-start(bf16[2,2,128,4,64]{2,4,1,0,3:T(8,128)(2,1)} %copy.69), calls=%async_computation.5 | async-start | bytes 524288 | tf_op jit(solution)/shard_map/all_to_all | solution.py:83
  25.9 1.0 copy.57
  26.9 3.9 %mul.38 = f32[2,2,512,4,128]{4,3,2,1,0:T(4,128)} broadcast(f32[2,2,512,4]{3,2,1,0:T(8,128)S(1)} %copy.57), dimensions={0,1,2,3} | broadcast | bytes 4227072 | tf_op jit(solution)/shard_map/mul | solution.py:16
  30.8 5.6 %mul.39 = f32[2,2,512,512]{3,2,1,0:T(8,128)} reshape(f32[2,2,512,4,128]{4,3,2,1,0:T(4,128)} %mul.38) | data formatting | bytes 8388608 | tf_op jit(solution)/shard_map/mul | solution.py:16
  36.4 2.2 %copy.63 = bf16[2,2,512,512]{3,1,2,0:T(2,128)(2,1)S(1)} copy(bf16[2,2,512,512]{3,2,1,0:T(8,128)(2,1)S(1)} %copy-done.2) | data formatting | bytes 4194304 | tf_op args[0]
  38.6 0.0 copy-start.4
  38.6 0.0 copy-start.6
  38.6 2.0 copy.64
  40.6 1.7 all-to-all-done.5
  42.3 4.5 %all-to-all-start.3 = ((bf16[2,2,128,4,512]{4,2,1,0,3:T(8,128)(2,1)}), bf16[2,2,128,4,512]{4,2,1,0,3:T(8,128)(2,1)}, u32[]{:S(2)}, u32[]{:S(2)}) async-start(bf16[2,2,128,4,512]{4,2,1,0,3:T(8,128)(2,1)} %copy.64), calls=%async_computation.3 | async-start | bytes 4194304 | tf_op jit(solution)/shard_map/all_to_all | solution.py:81
  46.8 71.2 %all_gather.7 = bf16[2,2,4,128,64]{4,3,2,1,0:T(8,128)(2,1)S(1)} all-gather(bf16[2,2,4,32,64]{4,3,2,1,0:T(8,128)(2,1)S(1)} %copy-done.4), channel_id=1, replica_groups=mesh['group'=2,'seq'=4,'req'=2,'sub'=2] {'seq'}, dimensions={3}, use_global_device_ids=true | all-gather | bytes 327680 | tf_op jit(solution)/shard_map/all_gather | solution.py:72
  118.0 0.1 broadcast_compare_fusion
  118.1 0.2 fusion.17
  118.3 2.8 %fusion.16 = f32[2,2,512,512]{2,3,1,0:T(8,128)} fusion(bf16[2,2,512,64]{3,2,1,0:T(8,128)(2,1)S(1)} %bitcast.77, bf16[2,2,512,64]{2,3,1,0:T(8,128)(2,1)S(1)} %copy-done.3), kind=kOutput, calls=%fused_computation.39 | convolution fusion | flops 134217728 | bytes 4718592 | tf_op jit(solution)/shard_map/vmap(vmap())/dot_general | solution.py:28
  121.1 2.3 %fusion.15 = (bf16[2,2,512]{2,1,0:T(2,128)(2,1)S(1)}, f32[2,2,512,4]{2,3,1,0:T(4,128)S(1)}) fusion(f32[2,2,512,4]{2,3,1,0:T(4,128)S(1)} %fusion.17, bf16[2,2,512,512]{3,2,1,0:T(8,128)(2,1)} %bitcast.74, bf16[2,2,4,512]{3,2,1,0:T(4,128)(2,1)S(1)} %copy-done, pred[512,4]{0,1:T(4,128)(4,1)S(1)} %fusion.8), kind=kOutput, calls=%fused_computation.38 | convolution fusion | flops 8419328 | bytes 2185216 | tf_op jit(solution)/shard_map/vmap(vmap())/dot_general | solution.py:30
  123.4 5.6 %fusion.14 = (bf16[2,2,512]{2,1,0:T(2,128)(2,1)S(1)}, f32[2,2,512,512]{2,3,1,0:T(8,128)S(1)}) fusion(f32[2,2,512,512]{2,3,1,0:T(8,128)} %fusion.16, bf16[2,2,512,512]{3,2,1,0:T(8,128)(2,1)} %bitcast.75, f32[2,2,512,512]{3,2,1,0:T(8,128)} %mul.39, bf16[2,2,512,512]{3,2,1,0:T(8,128)(2,1)S(1)} %copy-done.2, pred[2,512]{1,0:T(4,128)(4,1)S(1)} %broadcast_compare_fusion), kind=kOutput, calls=%fused_computation.37 | convolution fusion | flops 1081079808 | bytes 16782336 | tf_op jit(solution)/shard_map/vmap(vmap())/dot_general | solution.py:26
  129.0 1.9 copy-done.1
  130.9 0.7 convert_reduce_fusion
  131.7 0.2 copy.62
  131.9 0.8 reshape.135
  132.7 5.0 %all-to-all-start.2 = ((bf16[4,2,256]{2,1,0:T(2,128)(2,1)}), bf16[4,2,256]{2,1,0:T(2,128)(2,1)S(1)}, u32[]{:S(2)}, u32[]{:S(2)}) async-start(bf16[4,2,256]{2,1,0:T(2,128)(2,1)} %reshape.135), calls=%async_computation.2 | async-start | bytes 8192 | tf_op jit(solution)/shard_map/all_to_all | solution.py:99
  137.6 7.1 %fusion.5 = f32[2,2,512,512]{3,2,1,0:T(8,128)} fusion(f32[2,2,512,512]{2,3,1,0:T(8,128)} %copy-done.1, f32[2,2,512]{2,1,0:T(2,128)S(1)} %get-tuple-element.20, pred[2,512]{1,0:T(4,128)(4,1)S(1)} %broadcast_compare_fusion, f32[2,2,512,512]{3,2,1,0:T(8,128)} %mul.39, bf16[2,2,512,512]{3,2,1,0:T(8,128)(2,1)S(1)} %copy-done.2), kind=kOutput, calls=%fused_computation.13 | convolution fusion | flops 1080033280 | bytes 14689280 | tf_op jit(solution)/shard_map/vmap(vmap())/dot_general | solution.py:45
  144.8 0.2 copy.59
  145.0 0.8 reshape.133
  145.7 5.1 %all-to-all-start = ((bf16[4,2,256]{2,1,0:T(2,128)(2,1)}), bf16[4,2,256]{2,1,0:T(2,128)(2,1)S(1)}, u32[]{:S(2)}, u32[]{:S(2)}) async-start(bf16[4,2,256]{2,1,0:T(2,128)(2,1)} %reshape.133), calls=%async_computation | async-start | bytes 8192 | tf_op jit(solution)/shard_map/all_to_all | solution.py:98
  150.8 3.0 %add_convert_fusion = bf16[2,2,512,512]{3,2,1,0:T(8,128)(2,1)S(1)} fusion(f32[2,2,512,512]{3,2,1,0:T(8,128)} %fusion.5, bf16[2,2,4,512]{3,2,1,0:T(4,128)(2,1)S(1)} %copy-done, f32[2,2,512,4]{2,3,1,0:T(4,128)S(1)} %get-tuple-element.27, f32[2,2,512]{2,1,0:T(2,128)S(1)} %get-tuple-element.20, pred[512,4]{0,1:T(4,128)(4,1)S(1)} %fusion.8), kind=kOutput, calls=%fused_computation.6 | convolution fusion | flops 10510336 | bytes 6350848 | tf_op jit(solution)/shard_map/vmap(vmap())/dot_general | solution.py:46
  153.8 3.0 %copy.61 = bf16[1,2,2,4,128,512]{5,3,2,1,0,4:T(4,128)(2,1)} copy(bf16[1,2,2,4,128,512]{5,4,3,2,1,0:T(8,128)(2,1)S(1)} %bitcast.72) | data formatting | bytes 4194304 | tf_op jit(solution)/shard_map/broadcast_in_dim;vmap(vmap())/reshape | solution.py:97
  156.8 5.1 %all-to-all-start.1 = ((bf16[1,2,2,4,128,512]{5,3,2,1,0,4:T(4,128)(2,1)}), bf16[1,2,2,4,128,512]{5,3,2,1,0,4:T(4,128)(2,1)S(1)}, u32[]{:S(2)}, u32[]{:S(2)}) async-start(bf16[1,2,2,4,128,512]{5,3,2,1,0,4:T(4,128)(2,1)} %copy.61), calls=%async_computation.1 | async-start | bytes 4194304 | tf_op jit(solution)/shard_map/all_to_all | solution.py:97
  161.9 0.6 copy_bitcast_fusion
  162.5 0.7 bitcast_bitcast_fusion
  163.2 3.1 %copy.65 = bf16[2,2,128,4,512]{4,2,3,1,0:T(8,128)(2,1)} copy(bf16[2,2,128,4,512]{4,2,1,0,3:T(8,128)(2,1)} %all-to-all-done.3) | data formatting | bytes 4194304 | tf_op jit(solution)/shard_map/all_to_all | solution.py:81
  166.3 0.3 reshape.134
  166.6 0.2 reduce_max.34
  166.8 0.3 reshape.136
  167.1 0.3 fusion.6
  167.4 38.4 %all-to-all-done.1 = bf16[1,2,2,4,128,512]{5,3,2,1,0,4:T(4,128)(2,1)S(1)} async-done(((bf16[1,2,2,4,128,512]{5,3,2,1,0,4:T(4,128)(2,1)}), bf16[1,2,2,4,128,512]{5,3,2,1,0,4:T(4,128)(2,1)S(1)}, u32[]{:S(2)}, u32[]{:S(2)}) %all-to-all-start.1) | async-done | bytes 2097184 | tf_op jit(solution)/shard_map/all_to_all | solution.py:97
  205.9 1.5 fusion
  207.4 0.3 divide_convert_fusion
  207.7 1.1 copy.71
  (23 shorter events, 0.2 us)
Async XLA Ops:
  7.2 113.9 %copy-start = (bf16[2,2,4,512]{3,2,1,0:T(4,128)(2,1)S(1)}, bf16[2,2,4,512]{3,2,1,0:T(4,128)(2,1)}, u32[]{:S(2)}) copy-start(bf16[2,2,4,512]{3,2,1,0:T(4,128)(2,1)} %param.14) | copy-start | bytes 49156
  7.2 113.9 %all-gather.2.cloned.1.call-start = ((), (), s32[]{:S(2)}) async-start(), calls=%async_computation.6 | async-start | bytes 2621440 | tf_op jit(solution)/shard_map/all_gather | solution.py:71
  10.6 11.9 %all-to-all-start.4 = ((bf16[2,2,128,4,4]{2,4,1,0,3:T(4,128)(2,1)}), bf16[2,2,128,4,4]{2,4,1,0,3:T(4,128)(2,1)S(1)}, u32[]{:S(2)}, u32[]{:S(2)}) async-start(bf16[2,2,128,4,4]{2,4,1,0,3:T(4,128)(2,1)} %copy.66), calls=%async_computation.4 | async-start | bytes 32768 | tf_op jit(solution)/shard_map/all_to_all | solution.py:82
  22.5 19.8 %all-to-all-start.5 = ((bf16[2,2,128,4,64]{2,4,1,0,3:T(8,128)(2,1)}), bf16[2,2,128,4,64]{2,4,1,0,3:T(8,128)(2,1)S(1)}, u32[]{:S(2)}, u32[]{:S(2)}) async-start(bf16[2,2,128,4,64]{2,4,1,0,3:T(8,128)(2,1)} %copy.69), calls=%async_computation.5 | async-start | bytes 524288 | tf_op jit(solution)/shard_map/all_to_all | solution.py:83
  30.8 5.6 %copy-start.2 = (bf16[2,2,512,512]{3,2,1,0:T(8,128)(2,1)S(1)}, bf16[2,2,512,512]{3,2,1,0:T(8,128)(2,1)}, u32[]{:S(2)}) copy-start(bf16[2,2,512,512]{3,2,1,0:T(8,128)(2,1)} %param.8) | copy-start | bytes 6291460
  38.6 8.2 %copy-start.4 = (bf16[2,2,4,32,64]{4,3,2,1,0:T(8,128)(2,1)S(1)}, bf16[2,2,4,32,64]{4,3,2,1,0:T(8,128)(2,1)}, u32[]{:S(2)}) copy-start(bf16[2,2,4,32,64]{4,3,2,1,0:T(8,128)(2,1)} %param.13) | copy-start | bytes 196612
  38.6 79.4 %copy-start.6 = (s32[2]{0:T(128)S(1)}, s32[2]{0:T(128)}, u32[]{:S(2)}) copy-start(s32[2]{0:T(128)} %param.11) | copy-start | bytes 28
  38.6 79.5 %copy-start.5 = (bf16[2,2,4,64]{3,2,1,0:T(4,128)(2,1)S(1)}, bf16[2,2,4,64]{3,2,1,0:T(4,128)(2,1)}, u32[]{:S(2)}) copy-start(bf16[2,2,4,64]{3,2,1,0:T(4,128)(2,1)} %param.15) | copy-start | bytes 6148
  38.6 79.7 %copy-start.3 = (bf16[2,2,512,64]{2,3,1,0:T(8,128)(2,1)S(1)}, bf16[2,2,512,64]{2,3,1,0:T(8,128)(2,1)}, u32[]{:S(2)}) copy-start(bf16[2,2,512,64]{2,3,1,0:T(8,128)(2,1)} %param.10) | copy-start | bytes 786436
  42.3 90.3 %all-to-all-start.3 = ((bf16[2,2,128,4,512]{4,2,1,0,3:T(8,128)(2,1)}), bf16[2,2,128,4,512]{4,2,1,0,3:T(8,128)(2,1)}, u32[]{:S(2)}, u32[]{:S(2)}) async-start(bf16[2,2,128,4,512]{4,2,1,0,3:T(8,128)(2,1)} %copy.64), calls=%async_computation.3 | async-start | bytes 4194304 | tf_op jit(solution)/shard_map/all_to_all | solution.py:81
  128.9 2.0 copy-start.1
  132.7 13.1 %all-to-all-start.2 = ((bf16[4,2,256]{2,1,0:T(2,128)(2,1)}), bf16[4,2,256]{2,1,0:T(2,128)(2,1)S(1)}, u32[]{:S(2)}, u32[]{:S(2)}) async-start(bf16[4,2,256]{2,1,0:T(2,128)(2,1)} %reshape.135), calls=%async_computation.2 | async-start | bytes 8192 | tf_op jit(solution)/shard_map/all_to_all | solution.py:99
  145.7 11.0 %all-to-all-start = ((bf16[4,2,256]{2,1,0:T(2,128)(2,1)}), bf16[4,2,256]{2,1,0:T(2,128)(2,1)S(1)}, u32[]{:S(2)}, u32[]{:S(2)}) async-start(bf16[4,2,256]{2,1,0:T(2,128)(2,1)} %reshape.133), calls=%async_computation | async-start | bytes 8192 | tf_op jit(solution)/shard_map/all_to_all | solution.py:98
  156.8 49.1 %all-to-all-start.1 = ((bf16[1,2,2,4,128,512]{5,3,2,1,0,4:T(4,128)(2,1)}), bf16[1,2,2,4,128,512]{5,3,2,1,0,4:T(4,128)(2,1)S(1)}, u32[]{:S(2)}, u32[]{:S(2)}) async-start(bf16[1,2,2,4,128,512]{5,3,2,1,0,4:T(4,128)(2,1)} %copy.61), calls=%async_computation.1 | async-start | bytes 4194304 | tf_op jit(solution)/shard_map/all_to_all | solution.py:97
Sparse Core Ops, SparseCore 0:
  9.6 73.4 all-gather.1
where the time goes:
time: 216 us
  blocking collectives  71.2 us (33%)
  waiting for transfers between devices  44.2 us (20%)
  local copies, waits for them, and re-layouts  32.4 us (15%)
  starting transfers between devices  29.4 us (14%)
  matrix products  20.9 us (10%)
  between operations  14.3 us (7%)
  other arithmetic  3.24 us (2%)
    all_gather x1, blocking collectives, per_device(): lax.all_gather(query_rope, 'seq', axis=3, tiled=True)  71.2 us
    all_to_all x1, waiting for transfers between devices, per_device(): lax.all_to_all(group_sum[None], 'seq', split_axis=4, concat_axis=0, tiled...  38.4 us
    mul x2, local copies, waits for them, and re-layouts, dequantize(): scaled = shaped * scale_values.astype(jnp.float32)[..., None]  9.47 us
    unnamed x22, local copies, waits for them, and re-layouts  9.29 us
    dot_general x1, matrix products, shard_partial(): group_sum = jnp.dot(weights, key_rows, preferred_element_type=jnp.float32)  7.14 us
    all_to_all x1, starting transfers between devices, per_device(): lax.all_to_all(regroup_rows(latent_scales), 'seq', split_axis=3, concat_a...  6.32 us
    reshape x4, local copies, waits for them, and re-layouts, regroup_rows(): values.reshape(values.shape[0], values.shape[1], span // shard_count, sha...  5.68 us
    dot_general x1, matrix products, shard_partial(): scores = jnp.dot(query_rows, key_rows.T, preferred_element_type=jnp.float32)  5.57 us
  transfers between devices with their start and end apart: 7, of which 3 were waited for; matrix products, arithmetic and copies ran while one was open for 24% of the time, Pallas kernels for 0%

commit v1 on v0

--- a/solution.py
+++ b/solution.py
@@ -64,12 +64,47 @@
 def per_device(
     latent_codes, latent_scales, rope_keys, lengths, query_latent, query_rope, new_latent, new_rope
 ):
+
+    def fill_fields(x_part, dev_axis, array_axis):
+        x_next = jax.lax.axis_size(dev_axis)
+        small = jax.lax.axis_index(dev_axis)
+        tmp, near, after = (x_next, small, x_part.shape[array_axis])
+        sheets = []
+        nth = 0
+        while nth < tmp:
+            sheets.append((nth, (nth + 1) % tmp))
+            nth = nth + 1
+        parts_seen = []
+        nth = 0
+        while nth < tmp:
+            parts_seen.append((nth, (nth - 1) % tmp))
+            nth += 1
+        now = jnp.zeros(
+            (*x_part.shape[:array_axis], tmp * after, *x_part.shape[array_axis + 1 :]), x_part.dtype
+        )
+        now = lax.dynamic_update_slice_in_dim(now, x_part, near * after, axis=array_axis)
+        local_part = met_up = x_part
+        outer = tmp // 2
+        i = 1
+        while i < outer + 1:
+            local_part = jax.lax.ppermute(local_part, dev_axis, sheets)
+            now = lax.dynamic_update_slice_in_dim(
+                now, local_part, (near - i) % tmp * after, axis=array_axis
+            )
+            if i < tmp - outer:
+                met_up = jax.lax.ppermute(met_up, dev_axis, parts_seen)
+                now = lax.dynamic_update_slice_in_dim(
+                    now, met_up, (near + i) % tmp * after, axis=array_axis
+                )
+            i = i + 1
+        return now
+
     shard_count = lax.axis_size("seq")
     seq_index = lax.axis_index("seq")
     layer_count, request_count, span, latent_width = latent_codes.shape
     lat_query, rope_query = (
         lax.all_gather(query_latent, "seq", axis=3, tiled=True),
-        lax.all_gather(query_rope, "seq", axis=3, tiled=True),
+        fill_fields(query_rope, "seq", 3),
     )
 
     def regroup_rows(values):

time: 216 us -> 357 us (1.65)
  local copies, waits for them, and re-layouts: 32.4 us -> 169 us
  blocking collectives: 71.2 us -> 0 us
  waiting for transfers between devices: 44.2 us -> 106 us
  starting transfers between devices: 29.4 us -> 43.8 us
    dynamic_update_slice x0 -> x4, local copies, waits for them, and re-layouts: none -> 133 us  [the longest x2 84 us: fill_fields(): lax.dynamic_update_slice_in_dim(now, local_part, (near - i) % tmp * after...]
    all_gather x1 -> x0, blocking collectives: 71.2 us -> none  [per_device(): lax.all_gather(query_rope, 'seq', axis=3, tiled=True)]
    ppermute x0 -> x3, waiting for transfers between devices: none -> 49.1 us  [the longest x2 49.1 us: fill_fields(): local_part = jax.lax.ppermute(local_part, dev_axis, sheets)]
    ppermute x0 -> x3, starting transfers between devices: none -> 15.5 us  [the longest x2 13.6 us: fill_fields(): local_part = jax.lax.ppermute(local_part, dev_axis, sheets)]
    all_to_all x1, waiting for transfers between devices: 1.7 us -> 12.2 us  [per_device(): lax.all_to_all(regroup_rows(rope_keys), 'seq', split_axis=3, concat_axis=...]
    unnamed x22 -> x35, local copies, waits for them, and re-layouts: 9.29 us -> 9.5 us
  transfers between devices with their start and end apart: 7 -> 10, of which waited for: 3 -> 4; matrix products, arithmetic and copies ran while one was open for 24% -> 53% of each run, Pallas kernels for 0% -> 0%
where the time goes in v1:
time: 357 us; the launch traced here: 356 us
  local copies, waits for them, and re-layouts  169 us (47%)
  waiting for transfers between devices  106 us (30%)
  starting transfers between devices  43.8 us (12%)
  matrix products  18 us (5%)
  between operations  14.5 us (4%)
  other arithmetic  4.41 us (1%)
    dynamic_update_slice x2, local copies, waits for them, and re-layouts, fill_fields(): lax.dynamic_update_slice_in_dim(now, local_part, (near - i) % tmp * after...  84 us
    ppermute x2, waiting for transfers between devices, fill_fields(): local_part = jax.lax.ppermute(local_part, dev_axis, sheets)  49.1 us
    dynamic_update_slice x1, local copies, waits for them, and re-layouts, fill_fields(): lax.dynamic_update_slice_in_dim(now, met_up, (near + i) % tmp * after, ax...  42 us
    all_to_all x1, waiting for transfers between devices, per_device(): lax.all_to_all(group_sum[None], 'seq', split_axis=4, concat_axis=0, tiled...  40.6 us
    ppermute x2, starting transfers between devices, fill_fields(): local_part = jax.lax.ppermute(local_part, dev_axis, sheets)  13.6 us
    all_to_all x1, waiting for transfers between devices, per_device(): lax.all_to_all(regroup_rows(rope_keys), 'seq', split_axis=3, concat_axis=...  12.2 us
    unnamed x35, local copies, waits for them, and re-layouts  9.5 us
    mul x2, local copies, waits for them, and re-layouts, dequantize(): scaled = shaped * scale_values.astype(jnp.float32)[..., None]  9.33 us
  transfers between devices with their start and end apart: 10, of which 4 were waited for; matrix products, arithmetic and copies ran while one was open for 53% of the time, Pallas kernels for 0%

profile of v1, /device:TPU:0, one launch (start us, length us, event | category | flops | bytes accessed | tf_op | source)
XLA Modules:
  0.0 356.1 jit_solution(3393466715288613389)
XLA Ops:
  7.2 0.7 all-gather.2.cloned.1.call-update
  7.9 1.8 reshape.126
  9.8 0.8 copy.84
  10.6 6.3 %all-to-all-start.4 = ((bf16[2,2,128,4,4]{2,4,1,0,3:T(4,128)(2,1)}), bf16[2,2,128,4,4]{2,4,1,0,3:T(4,128)(2,1)S(1)}, u32[]{:S(2)}, u32[]{:S(2)}) async-start(bf16[2,2,128,4,4]{2,4,1,0,3:T(4,128)(2,1)} %copy.84), calls=%async_computation.4 | async-start | bytes 32768 | tf_op jit(solution)/shard_map/all_to_all | solution.py:117
  16.9 1.2 copy.86
  18.2 1.0 copy.87
  19.2 3.4 all-to-all-done.4
  22.5 3.4 all-to-all-start.5
  26.0 2.2 copy.81
  28.2 2.0 copy.82
  30.1 12.2 %all-to-all-done.5 = bf16[2,2,128,4,64]{2,4,1,0,3:T(8,128)(2,1)S(1)} async-done(((bf16[2,2,128,4,64]{2,4,1,0,3:T(8,128)(2,1)}), bf16[2,2,128,4,64]{2,4,1,0,3:T(8,128)(2,1)S(1)}, u32[]{:S(2)}, u32[]{:S(2)}) %all-to-all-start.5) | async-done | bytes 262176 | tf_op jit(solution)/shard_map/all_to_all | solution.py:118
  42.3 4.5 %all-to-all-start.3 = ((bf16[2,2,128,4,512]{4,2,1,0,3:T(8,128)(2,1)}), bf16[2,2,128,4,512]{4,2,1,0,3:T(8,128)(2,1)}, u32[]{:S(2)}, u32[]{:S(2)}) async-start(bf16[2,2,128,4,512]{4,2,1,0,3:T(8,128)(2,1)} %copy.82), calls=%async_computation.3 | async-start | bytes 4194304 | tf_op jit(solution)/shard_map/all_to_all | solution.py:116
  46.8 2.0 collective-permute-start
  48.8 1.9 collective-permute-start.1
  50.7 0.6 broadcast_compare_fusion
  51.4 49.1 %collective-permute-done = bf16[2,2,4,32,64]{4,3,2,1,0:T(8,128)(2,1)} collective-permute-done((bf16[2,2,4,32,64]{4,3,2,1,0:T(8,128)(2,1)S(1)}, bf16[2,2,4,32,64]{4,3,2,1,0:T(8,128)(2,1)}, u32[]{:S(2)}, u32[]{:S(2)}) %collective-permute-start) | collective-permute-done | bytes 65568 | tf_op jit(solution)/shard_map/ppermute | solution.py:90
  100.4 11.7 %collective-permute-start.2 = (bf16[2,2,4,32,64]{4,3,2,1,0:T(8,128)(2,1)}, bf16[2,2,4,32,64]{4,3,2,1,0:T(8,128)(2,1)}, u32[]{:S(2)}, u32[]{:S(2)}) collective-permute-start(bf16[2,2,4,32,64]{4,3,2,1,0:T(8,128)(2,1)} %collective-permute-done), channel_id=1, source_target_pairs={{0,4},{4,8},{8,12},{12,0},{1,5},{5,9},{9,13},{13,1},{2,6},{6,10},{... | collective-permute-start | bytes 196616 | tf_op jit(solution)/shard_map/ppermute | solution.py:90
  112.1 0.6 fusion.8
  112.9 1.0 copy.72
  113.9 3.9 %mul.50 = f32[2,2,512,4,128]{4,3,2,1,0:T(4,128)} broadcast(f32[2,2,512,4]{3,2,1,0:T(8,128)S(1)} %copy.72), dimensions={0,1,2,3} | broadcast | bytes 4227072 | tf_op jit(solution)/shard_map/mul | solution.py:16
  117.8 5.5 %mul.51 = f32[2,2,512,512]{3,2,1,0:T(8,128)} reshape(f32[2,2,512,4,128]{4,3,2,1,0:T(4,128)} %mul.50) | data formatting | bytes 8388608 | tf_op jit(solution)/shard_map/mul | solution.py:16
  123.3 7.5 %dynamic_update_slice.12 = bf16[2,2,4,128,64]{3,2,4,1,0:T(4,128)(2,1)S(1)} dynamic-update-slice(bf16[2,2,4,128,64]{3,2,4,1,0:T(4,128)(2,1)S(1)} %broadcast_in_dim.45, bf16[2,2,4,32,64]{3,2,4,1,0:T(4,128)(2,1)S(1)} %copy.73, s32[]{:T(128)} %constant.52.clone.1, s32[]{:T(128)} %constant.52.clone.1, s32[]{:T(128)} %constant.52.clone.1, s32[]{:T(128)S(6)} %select_n.50, s32[]{:T(128)} %constant.52.clone.1) | dynamic-update-slice | bytes 131076 | tf_op jit(solution)/shard_map/dynamic_update_slice | solution.py:85
  130.8 1.1 copy.74
  131.9 42.0 %dynamic_update_slice.13 = bf16[2,2,4,128,64]{3,2,4,1,0:T(4,128)(2,1)S(1)} dynamic-update-slice(bf16[2,2,4,128,64]{3,2,4,1,0:T(4,128)(2,1)S(1)} %dynamic_update_slice.12, bf16[2,2,4,32,64]{3,2,4,1,0:T(4,128)(2,1)S(1)} %copy.74, s32[]{:T(128)} %constant.52.clone.1, s32[]{:T(128)} %constant.52.clone.1, s32[]{:T(128)} %constant.52.clone.1, s32[]{:T(128)S(6)} %select_n.52, s32[]{:T(128)} %constant.52.clone.1) | dynamic-update-slice | bytes 131076 | tf_op jit(solution)/shard_map/dynamic_update_slice | solution.py:91
  173.9 1.1 copy.75
  175.0 42.0 %dynamic_update_slice.14 = bf16[2,2,4,128,64]{3,2,4,1,0:T(4,128)(2,1)S(1)} dynamic-update-slice(bf16[2,2,4,128,64]{3,2,4,1,0:T(4,128)(2,1)S(1)} %dynamic_update_slice.13, bf16[2,2,4,32,64]{3,2,4,1,0:T(4,128)(2,1)S(1)} %copy.75, s32[]{:T(128)} %constant.52.clone.1, s32[]{:T(128)} %constant.52.clone.1, s32[]{:T(128)} %constant.52.clone.1, s32[]{:T(128)S(6)} %select_n.54, s32[]{:T(128)} %constant.52.clone.1) | dynamic-update-slice | bytes 131076 | tf_op jit(solution)/shard_map/dynamic_update_slice | solution.py:96
  217.0 1.1 copy.76
  218.1 42.0 %dynamic_update_slice.15 = bf16[2,2,4,128,64]{3,2,4,1,0:T(4,128)(2,1)S(1)} dynamic-update-slice(bf16[2,2,4,128,64]{3,2,4,1,0:T(4,128)(2,1)S(1)} %dynamic_update_slice.14, bf16[2,2,4,32,64]{3,2,4,1,0:T(4,128)(2,1)S(1)} %copy.76, s32[]{:T(128)} %constant.52.clone.1, s32[]{:T(128)} %constant.52.clone.1, s32[]{:T(128)} %constant.52.clone.1, s32[]{:T(128)S(6)} %select_n.56, s32[]{:T(128)} %constant.52.clone.1) | dynamic-update-slice | bytes 131076 | tf_op jit(solution)/shard_map/dynamic_update_slice | solution.py:91
  260.3 2.2 fusion.17
  262.7 4.2 %fusion.13 = f32[2,2,512,512]{3,2,1,0:T(8,128)S(1)} fusion(bf16[2,2,512,512]{3,2,1,0:T(8,128)(2,1)} %bitcast.76, f32[2,2,512,512]{3,2,1,0:T(8,128)} %mul.51, bf16[2,2,512,512]{3,2,1,0:T(8,128)(2,1)S(1)} %copy-done.2), kind=kOutput, calls=%fused_computation.36 | convolution fusion | flops 1076887552 | bytes 12582912 | tf_op jit(solution)/shard_map/vmap(vmap())/dot_general | solution.py:26
  266.9 1.3 fusion.15
  268.3 1.9 copy-done.1
  270.2 0.8 convert_reduce_fusion
  271.2 0.8 reshape.135
  272.0 3.9 %all-to-all-start.2 = ((bf16[4,2,256]{2,1,0:T(2,128)(2,1)}), bf16[4,2,256]{2,1,0:T(2,128)(2,1)S(1)}, u32[]{:S(2)}, u32[]{:S(2)}) async-start(bf16[4,2,256]{2,1,0:T(2,128)(2,1)} %reshape.135), calls=%async_computation.2 | async-start | bytes 8192 | tf_op jit(solution)/shard_map/all_to_all | solution.py:134
  275.8 7.2 %fusion.5 = f32[2,2,512,512]{3,2,1,0:T(8,128)} fusion(f32[2,2,512,512]{2,3,1,0:T(8,128)} %copy-done.1, f32[2,2,512]{2,1,0:T(2,128)S(1)} %get-tuple-element.20, pred[2,512]{1,0:T(4,128)(4,1)S(1)} %copy-done.7, f32[2,2,512,512]{3,2,1,0:T(8,128)} %mul.51, bf16[2,2,512,512]{3,2,1,0:T(8,128)(2,1)S(1)} %copy-done.2), kind=kOutput, calls=%fused_computation.13 | convolution fusion | flops 1080033280 | bytes 14689280 | tf_op jit(solution)/shard_map/vmap(vmap())/dot_general | solution.py:45
  283.2 0.8 reshape.133
  284.0 5.1 %all-to-all-start = ((bf16[4,2,256]{2,1,0:T(2,128)(2,1)}), bf16[4,2,256]{2,1,0:T(2,128)(2,1)S(1)}, u32[]{:S(2)}, u32[]{:S(2)}) async-start(bf16[4,2,256]{2,1,0:T(2,128)(2,1)} %reshape.133), calls=%async_computation | async-start | bytes 8192 | tf_op jit(solution)/shard_map/all_to_all | solution.py:133
  289.0 3.0 add_convert_fusion
  292.0 3.0 copy.79
  295.0 5.1 %all-to-all-start.1 = ((bf16[1,2,2,4,128,512]{5,3,2,1,0,4:T(4,128)(2,1)}), bf16[1,2,2,4,128,512]{5,3,2,1,0,4:T(4,128)(2,1)S(1)}, u32[]{:S(2)}, u32[]{:S(2)}) async-start(bf16[1,2,2,4,128,512]{5,3,2,1,0,4:T(4,128)(2,1)} %copy.79), calls=%async_computation.1 | async-start | bytes 4194304 | tf_op jit(solution)/shard_map/all_to_all | solution.py:132
  300.1 0.6 copy_bitcast_fusion
  300.7 0.7 bitcast_bitcast_fusion
  301.4 3.1 copy.83
  305.4 0.3 fusion.6
  305.7 40.6 %all-to-all-done.1 = bf16[1,2,2,4,128,512]{5,3,2,1,0,4:T(4,128)(2,1)S(1)} async-done(((bf16[1,2,2,4,128,512]{5,3,2,1,0,4:T(4,128)(2,1)}), bf16[1,2,2,4,128,512]{5,3,2,1,0,4:T(4,128)(2,1)S(1)}, u32[]{:S(2)}, u32[]{:S(2)}) %all-to-all-start.1) | async-done | bytes 2097184 | tf_op jit(solution)/shard_map/all_to_all | solution.py:132
  346.3 1.5 fusion
  348.2 1.1 copy.89
  (50 shorter events, 2.2 us)
Async XLA Ops:
  7.2 253.1 %copy-start = (bf16[2,2,4,512]{3,2,1,0:T(4,128)(2,1)S(1)}, bf16[2,2,4,512]{3,2,1,0:T(4,128)(2,1)}, u32[]{:S(2)}) copy-start(bf16[2,2,4,512]{3,2,1,0:T(4,128)(2,1)} %param.14) | copy-start | bytes 49156
  7.2 18.8 %copy-start.2 = (bf16[2,2,512,512]{3,2,1,0:T(8,128)(2,1)S(1)}, bf16[2,2,512,512]{3,2,1,0:T(8,128)(2,1)}, u32[]{:S(2)}) copy-start(bf16[2,2,512,512]{3,2,1,0:T(8,128)(2,1)} %param.8) | copy-start | bytes 6291460
  7.2 253.1 %all-gather.2.cloned.1.call-start = ((), (), s32[]{:S(2)}) async-start(), calls=%async_computation.6 | async-start | bytes 2621440 | tf_op jit(solution)/shard_map/all_gather | solution.py:106
  10.6 11.9 %all-to-all-start.4 = ((bf16[2,2,128,4,4]{2,4,1,0,3:T(4,128)(2,1)}), bf16[2,2,128,4,4]{2,4,1,0,3:T(4,128)(2,1)S(1)}, u32[]{:S(2)}, u32[]{:S(2)}) async-start(bf16[2,2,128,4,4]{2,4,1,0,3:T(4,128)(2,1)} %copy.84), calls=%async_computation.4 | async-start | bytes 32768 | tf_op jit(solution)/shard_map/all_to_all | solution.py:117
  22.5 7.6 %copy-start.8 = (bf16[2,2,128,4,4]{2,4,1,0,3:T(4,128)(2,1)}, bf16[2,2,128,4,4]{2,4,1,0,3:T(4,128)(2,1)S(1)}, u32[]{:S(2)}) copy-start(bf16[2,2,128,4,4]{2,4,1,0,3:T(4,128)(2,1)S(1)} %all-to-all-done.4) | copy-start | bytes 49156
  22.5 19.8 %all-to-all-start.5 = ((bf16[2,2,128,4,64]{2,4,1,0,3:T(8,128)(2,1)}), bf16[2,2,128,4,64]{2,4,1,0,3:T(8,128)(2,1)S(1)}, u32[]{:S(2)}, u32[]{:S(2)}) async-start(bf16[2,2,128,4,64]{2,4,1,0,3:T(8,128)(2,1)} %copy.87), calls=%async_computation.5 | async-start | bytes 524288 | tf_op jit(solution)/shard_map/all_to_all | solution.py:118
  28.1 18.7 %copy-start.6 = (bf16[2,2,4,32,64]{4,3,2,1,0:T(8,128)(2,1)S(1)}, bf16[2,2,4,32,64]{4,3,2,1,0:T(8,128)(2,1)}, u32[]{:S(2)}) copy-start(bf16[2,2,4,32,64]{4,3,2,1,0:T(8,128)(2,1)} %param.13) | copy-start | bytes 196612
  28.1 22.6 %copy-start.12 = (s32[2]{0:T(128)S(1)}, s32[2]{0:T(128)}, u32[]{:S(2)}) copy-start(s32[2]{0:T(128)} %param.11) | copy-start | bytes 28
  42.3 70.6 %copy-start.4 = (bf16[2,2,128,4,64]{2,4,1,0,3:T(8,128)(2,1)}, bf16[2,2,128,4,64]{2,4,1,0,3:T(8,128)(2,1)S(1)}, u32[]{:S(2)}) copy-start(bf16[2,2,128,4,64]{2,4,1,0,3:T(8,128)(2,1)S(1)} %all-to-all-done.5) | copy-start | bytes 786436
  42.3 229.6 %all-to-all-start.3 = ((bf16[2,2,128,4,512]{4,2,1,0,3:T(8,128)(2,1)}), bf16[2,2,128,4,512]{4,2,1,0,3:T(8,128)(2,1)}, u32[]{:S(2)}, u32[]{:S(2)}) async-start(bf16[2,2,128,4,512]{4,2,1,0,3:T(8,128)(2,1)} %copy.82), calls=%async_computation.3 | async-start | bytes 4194304 | tf_op jit(solution)/shard_map/all_to_all | solution.py:116
  46.8 53.6 %collective-permute-start = (bf16[2,2,4,32,64]{4,3,2,1,0:T(8,128)(2,1)S(1)}, bf16[2,2,4,32,64]{4,3,2,1,0:T(8,128)(2,1)}, u32[]{:S(2)}, u32[]{:S(2)}) collective-permute-start(bf16[2,2,4,32,64]{4,3,2,1,0:T(8,128)(2,1)S(1)} %copy-done.6), channel_id=1, source_target_pairs={{0,4},{4,8},{8,12},{12,0},{1,5},{5,9},{9,13},{13,1},{2,6},{6,10},{... | collective-permute-start | bytes 196616 | tf_op jit(solution)/shard_map/ppermute | solution.py:90
  48.8 125.1 %collective-permute-start.1 = (bf16[2,2,4,32,64]{4,3,2,1,0:T(8,128)(2,1)S(1)}, bf16[2,2,4,32,64]{4,3,2,1,0:T(8,128)(2,1)}, u32[]{:S(2)}, u32[]{:S(2)}) collective-permute-start(bf16[2,2,4,32,64]{4,3,2,1,0:T(8,128)(2,1)S(1)} %copy-done.6), channel_id=1, source_target_pairs={{0,12},{4,0},{8,4},{12,8},{1,13},{5,1},{9,5},{13,9},{2,14},{6,2},{... | collective-permute-start | bytes 196616 | tf_op jit(solution)/shard_map/ppermute | solution.py:95
  100.4 116.6 %collective-permute-start.2 = (bf16[2,2,4,32,64]{4,3,2,1,0:T(8,128)(2,1)}, bf16[2,2,4,32,64]{4,3,2,1,0:T(8,128)(2,1)}, u32[]{:S(2)}, u32[]{:S(2)}) collective-permute-start(bf16[2,2,4,32,64]{4,3,2,1,0:T(8,128)(2,1)} %collective-permute-done), channel_id=1, source_target_pairs={{0,4},{4,8},{8,12},{12,0},{1,5},{5,9},{9,13},{13,1},{2,6},{6,10},{... | collective-permute-start | bytes 196616 | tf_op jit(solution)/shard_map/ppermute | solution.py:90
  123.2 139.3 %copy-start.10 = (pred[512,4]{0,1:T(4,128)(4,1)S(1)}, pred[512,4]{0,1:T(4,128)(4,1)}, u32[]{:S(2)}) copy-start(pred[512,4]{0,1:T(4,128)(4,1)} %fusion.8) | copy-start | bytes 6148
  123.2 139.3 %copy-start.11 = (bf16[2,2,4,64]{3,2,1,0:T(4,128)(2,1)S(1)}, bf16[2,2,4,64]{3,2,1,0:T(4,128)(2,1)}, u32[]{:S(2)}) copy-start(bf16[2,2,4,64]{3,2,1,0:T(4,128)(2,1)} %param.15) | copy-start | bytes 6148
  262.7 4.2 %copy-start.3 = (bf16[2,2,512,64]{2,3,1,0:T(8,128)(2,1)S(1)}, bf16[2,2,512,64]{2,3,1,0:T(8,128)(2,1)}, u32[]{:S(2)}) copy-start(bf16[2,2,512,64]{2,3,1,0:T(8,128)(2,1)} %param.10) | copy-start | bytes 786436
  262.7 4.2 %copy-start.7 = (pred[2,512]{1,0:T(4,128)(4,1)S(1)}, pred[2,512]{1,0:T(4,128)(4,1)}, u32[]{:S(2)}) copy-start(pred[2,512]{1,0:T(4,128)(4,1)} %broadcast_compare_fusion) | copy-start | bytes 3076
  268.2 2.0 copy-start.1
  272.0 12.0 %all-to-all-start.2 = ((bf16[4,2,256]{2,1,0:T(2,128)(2,1)}), bf16[4,2,256]{2,1,0:T(2,128)(2,1)S(1)}, u32[]{:S(2)}, u32[]{:S(2)}) async-start(bf16[4,2,256]{2,1,0:T(2,128)(2,1)} %reshape.135), calls=%async_computation.2 | async-start | bytes 8192 | tf_op jit(solution)/shard_map/all_to_all | solution.py:134
  284.0 11.0 %all-to-all-start = ((bf16[4,2,256]{2,1,0:T(2,128)(2,1)}), bf16[4,2,256]{2,1,0:T(2,128)(2,1)S(1)}, u32[]{:S(2)}, u32[]{:S(2)}) async-start(bf16[4,2,256]{2,1,0:T(2,128)(2,1)} %reshape.133), calls=%async_computation | async-start | bytes 8192 | tf_op jit(solution)/shard_map/all_to_all | solution.py:133
  292.0 8.1 %copy-start.9 = (bf16[2,2,128,4,4]{2,4,1,0,3:T(4,128)(2,1)S(1)}, bf16[2,2,128,4,4]{2,4,1,0,3:T(4,128)(2,1)}, u32[]{:S(2)}) copy-start(bf16[2,2,128,4,4]{2,4,1,0,3:T(4,128)(2,1)} %copy-done.8) | copy-start | bytes 49156
  292.0 8.7 %copy-start.5 = (bf16[2,2,128,4,64]{2,4,1,0,3:T(8,128)(2,1)S(1)}, bf16[2,2,128,4,64]{2,4,1,0,3:T(8,128)(2,1)}, u32[]{:S(2)}) copy-start(bf16[2,2,128,4,64]{2,4,1,0,3:T(8,128)(2,1)} %copy-done.4) | copy-start | bytes 786436
  295.0 51.3 %all-to-all-start.1 = ((bf16[1,2,2,4,128,512]{5,3,2,1,0,4:T(4,128)(2,1)}), bf16[1,2,2,4,128,512]{5,3,2,1,0,4:T(4,128)(2,1)S(1)}, u32[]{:S(2)}, u32[]{:S(2)}) async-start(bf16[1,2,2,4,128,512]{5,3,2,1,0,4:T(4,128)(2,1)} %copy.79), calls=%async_computation.1 | async-start | bytes 4194304 | tf_op jit(solution)/shard_map/all_to_all | solution.py:132
Sparse Core Ops, SparseCore 0:
  9.6 73.4 all-gather.1
